TPU v7x, 128 devices: a whole 4x4x4 slice. The times are simulated.
128 devices in a mesh: tm: 4 (over z_hi, core), pair: 32 (over z_lo, y, x).
Axes of the slice: x: 4, y: 4, z: 4 (z_hi: 2, z_lo: 2; z = z_hi * 2 + z_lo), core: 2. Of those that a mesh axis runs over, the one named last changes fastest.
Arguments:
- orbitals: bfloat16 [32768, 512], P('pair', 'tm'), may hold values from -1.5 to 1.5
- level_gap: float32 [512], replicated, may hold values from 0.05 to 1.5
- screened: bfloat16 [8, 128, 1024, 1024], P('tm', 'pair'), may hold values from -0.008972168 to 0.008972168
- pair_blocks: int32 [128, 2], P('pair'), may hold values from 0 to 31, as said below
Outputs:
- self_energy: float32 [8, 512, 512], P('tm', 'pair')
Inputs may be any that keep to these rules, and one draw needn't show every extreme that they name: `pair_blocks`: each row names two point blocks a <= c; no unordered pair appears in two rows; the pair (0, 31) appears in every draw.
All inputs are finite; a program needn't handle non-finite values.
Results may differ from a plain program's by a relative error of at most 0.0049.
Values may be sent and summed in bfloat16 or wider, within the bound.
No kernel may reach another device: no remote copies, remote signals or barrier semaphores. Data moves between devices by JAX's collectives and lax.ppermute only.
A program may use at most 128 MiB of HBM per device.

v0:
```python
import jax
import jax.numpy as jnp
from jax import lax
from jax.sharding import Mesh
from jax.sharding import PartitionSpec as P

NOCC = 128
PAIR = ("pair_0", "pair_1", "pair_2")


def laid_out(tiles, dim):
    tiles = jnp.moveaxis(tiles, 0, dim)
    shape = tiles.shape
    return tiles.reshape(*shape[:dim], shape[dim] * shape[dim + 1], *shape[dim + 2 :])


def stacked_from(array, axes, sequence):
    tiles = array[None]
    for k in sequence:
        tiles = lax.all_gather(tiles, axes[k], axis=0, tiled=True)
    carried = [lax.axis_size(axes[k]) for k in reversed(sequence)]
    tiles = tiles.reshape(*carried, *array.shape)
    turned = sorted(range(len(sequence)), key=lambda place: sequence[len(sequence) - 1 - place])
    return tiles.transpose(*turned, *range(len(sequence), tiles.ndim)).reshape(-1, *array.shape)


def whole_of(array, axes, sequence, dim):
    return laid_out(stacked_from(array, axes, sequence), dim)


def split_up(array, dim, count):
    shape = array.shape
    tiles = array.reshape(*shape[:dim], count, shape[dim] // count, *shape[dim + 1 :])
    return jnp.moveaxis(tiles, dim, 0)


def sum_at_owner(array, axis, dim):
    count = lax.axis_size(axis)
    tiles = lax.all_to_all(split_up(array, dim, count), axis, 0, 0, tiled=True)
    return jnp.sum(tiles, axis=0)


def shards(orbitals, level_gap, screened, pair_blocks):
    block_rows = orbitals.shape[0]
    wanted = pair_blocks.reshape(-1)
    narrow = whole_of(orbitals, PAIR, (0, 1, 2), 0)
    picked = jnp.take(narrow.reshape(-1, block_rows, narrow.shape[1]), wanted, axis=0)
    chosen = lax.all_gather(picked, "tm", axis=2, tiled=True)
    orbital_count = chosen.shape[2]
    time_local = screened.shape[0]
    pair_local = screened.shape[1]
    time_total = time_local * lax.axis_size("tm")
    first_time = lax.axis_index("tm") * time_local
    moments = (first_time + jnp.arange(time_local)).astype(jnp.float32)
    tau = 6.0 * (moments + 0.5) / time_total
    signs = jnp.where(jnp.arange(orbital_count) < NOCC, 1.0, -1.0).astype(jnp.float32)
    factors = signs[None, :] * jnp.exp(-level_gap[None, :] * tau[:, None])
    totals = []
    for time_step in range(time_local):
        total = jnp.zeros((orbital_count, orbital_count), jnp.float32)
        for pair_step in range(pair_local):
            left = chosen[2 * pair_step]
            right = chosen[2 * pair_step + 1]
            scaled = (left.astype(jnp.float32) * factors[time_step][None, :]).astype(jnp.bfloat16)
            green = lax.dot_general(
                scaled, right, (((1,), (1,)), ((), ())), preferred_element_type=jnp.float32
            )
            product = (green * screened[time_step, pair_step].astype(jnp.float32)).astype(
                jnp.bfloat16
            )
            half = lax.dot_general(
                left, product, (((0,), (0,)), ((), ())), preferred_element_type=jnp.float32
            ).astype(jnp.bfloat16)
            block = jnp.dot(half, right, preferred_element_type=jnp.float32)
            weight = jnp.where(
                pair_blocks[pair_step, 0] == pair_blocks[pair_step, 1], 0.5, 1.0
            ).astype(jnp.float32)
            total = total + weight * (block + block.T)
        totals.append(total)
    partial_sum = jnp.stack(totals, axis=0)
    return sum_at_owner(partial_sum, PAIR, 1)


def solution(mesh):
    finer = Mesh(
        mesh.devices.reshape(mesh.shape["tm"], 2, 4, 4), ("tm", "pair_0", "pair_1", "pair_2")
    )
    placed = (P(PAIR, "tm"), P(), P("tm", PAIR, None, None), P(PAIR, None))
    return jax.shard_map(
        shards, mesh=finer, in_specs=placed, out_specs=P("tm", PAIR, None), check_vma=False
    )
```

profile of v0, /device:TPU:0, one launch (start us, length us, event | category | flops | bytes accessed | tf_op | source)
XLA Modules:
  0.0 349.6 jit_solution(2108790576608835699)
XLA Ops:
  6.5 10.9 %all-gather = bf16[2048,128]{1,0:T(8,128)(2,1)} all-gather(bf16[1024,128]{1,0:T(8,128)(2,1)} %param.4), channel_id=2, replica_groups=mesh['tm'=4,'pair_0'=2,'pair_1'=4,'pair_2'=4] {'pair_0'}, dimensions={0}, use_global_device_ids=true | all-gather | bytes 786432 | tf_op jit(solution)/shard_map/all_gather | solution.py:20
  17.5 0.0 all-gather.5.cloned.1.call-update
  17.5 0.0 all-gather.7.cloned.1.call-start
  17.6 32.8 %all-gather.5.cloned.1.call-done = bf16[8,1024,128]{2,1,0:T(8,128)(2,1)} async-done(((bf16[2,1024,128]{2,1,0:T(8,128)(2,1)}), bf16[8,1024,128]{2,1,0:T(8,128)(2,1)}) %all-gather.5.cloned.1.call-update) | async-done | bytes 2097168 | tf_op jit(solution)/shard_map/all_gather | solution.py:20
  50.4 0.0 all-gather.9.cloned.1.call-start
  50.4 0.8 copy.36
  51.2 0.1 reshape.151
  51.3 0.1 reshape.149
  51.4 83.7 %all-gather.7.cloned.1.call-done = bf16[32,1024,128]{2,1,0:T(8,128)(2,1)} async-done(((bf16[8,1024,128]{2,1,0:T(8,128)(2,1)}), bf16[32,1024,128]{2,1,0:T(8,128)(2,1)}) %all-gather.7.cloned.1.call-update) | async-done | bytes 8388624 | tf_op jit(solution)/shard_map/all_gather | solution.py:20
  135.1 7.5 %copy.37 = bf16[2,4,4,1024,128]{4,3,2,1,0:T(8,128)(2,1)} copy(bf16[2,4,4,1024,128]{4,3,0,1,2:T(8,128)(2,1)} %bitcast.218) | data formatting | bytes 16777216 | tf_op jit(solution)/shard_map/transpose | solution.py:24
  142.6 4.3 %gather_fusion = bf16[8,1024,128]{2,1,0:T(8,128)(2,1)S(1)} fusion(bf16[32,1024,128]{2,1,0:T(8,128)(2,1)} %bitcast.217, s32[1024]{0:T(1024)S(1)} %pad_clamp_fusion), kind=kCustom, calls=%fused_computation | custom fusion | bytes 4194336 | tf_op jit(solution)/shard_map/jit(_take)/gather | solution.py:47
  147.0 1.7 broadcast_select_fusion
  148.7 0.7 fusion.113
  154.4 0.1 exponential_multiply_fusion
  154.5 58.9 %all-gather.9.cloned.1.call-done = bf16[8,1024,512]{2,1,0:T(8,128)(2,1)} async-done(((bf16[8,1024,128]{2,1,0:T(8,128)(2,1)}), bf16[8,1024,512]{2,1,0:T(8,128)(2,1)}) %all-gather.9.cloned.1.call-update) | async-done | bytes 8388624 | tf_op jit(solution)/shard_map/all_gather | solution.py:48
  213.4 4.9 %convolution_convert_fusion.3 = bf16[512,1024]{1,0:T(8,128)(2,1)S(1)} fusion(bf16[2,4,1024,1024]{3,2,1,0:T(8,128)(2,1)} %param.6, f32[512]{0:T(512)S(1)} %bitcast.226, bf16[8,1024,512]{2,1,0:T(8,128)(2,1)} %all-gather.9.cloned.1.call-done), kind=kOutput, calls=%fused_computation.38 | convolution fusion | flops 2152726528 | bytes 6293504 | tf_op jit(solution)/shard_map/dot_general | solution.py:71
  218.3 1.9 fusion.102
  220.2 0.3 copy.43
  220.6 6.0 %convolution_convert_fusion.2 = bf16[512,1024]{1,0:T(8,128)(2,1)} fusion(bf16[2,4,1024,1024]{3,2,1,0:T(8,128)(2,1)} %param.6, f32[512]{0:T(512)S(1)} %bitcast.227, bf16[8,1024,512]{2,1,0:T(8,128)(2,1)} %all-gather.9.cloned.1.call-done), kind=kOutput, calls=%fused_computation.37 | convolution fusion | flops 2152726528 | bytes 6293504 | tf_op jit(solution)/shard_map/dot_general | solution.py:71
  226.5 2.2 fusion.104
  228.8 1.4 copy.44
  230.2 5.9 %convolution_convert_fusion = bf16[512,1024]{1,0:T(8,128)(2,1)} fusion(bf16[2,4,1024,1024]{3,2,1,0:T(8,128)(2,1)} %param.6, f32[512]{0:T(512)S(1)} %bitcast.228, bf16[8,1024,512]{2,1,0:T(8,128)(2,1)} %all-gather.9.cloned.1.call-done), kind=kOutput, calls=%fused_computation.35 | convolution fusion | flops 2152726528 | bytes 6293504 | tf_op jit(solution)/shard_map/dot_general | solution.py:71
  236.1 3.2 fusion.108
  239.3 2.5 copy.46
  241.8 6.0 %convolution_convert_fusion.1 = bf16[512,1024]{1,0:T(8,128)(2,1)} fusion(bf16[2,4,1024,1024]{3,2,1,0:T(8,128)(2,1)} %param.6, f32[512]{0:T(512)S(1)} %bitcast.229, bf16[8,1024,512]{2,1,0:T(8,128)(2,1)} %all-gather.9.cloned.1.call-done), kind=kOutput, calls=%fused_computation.36 | convolution fusion | flops 2152726528 | bytes 6293504 | tf_op jit(solution)/shard_map/dot_general | solution.py:71
  247.8 3.2 fusion.106
  251.0 2.8 copy.45
  253.8 5.9 %convolution_convert_fusion.4 = bf16[512,1024]{1,0:T(8,128)(2,1)} fusion(bf16[2,4,1024,1024]{3,2,1,0:T(8,128)(2,1)} %param.6, f32[512]{0:T(512)S(1)} %bitcast.222, bf16[8,1024,512]{2,1,0:T(8,128)(2,1)} %all-gather.9.cloned.1.call-done), kind=kOutput, calls=%fused_computation.39 | convolution fusion | flops 2152726528 | bytes 6293504 | tf_op jit(solution)/shard_map/dot_general | solution.py:71
  259.7 3.2 fusion.109
  262.9 2.5 copy.42
  265.5 5.9 %convolution_convert_fusion.5 = bf16[512,1024]{1,0:T(8,128)(2,1)} fusion(bf16[2,4,1024,1024]{3,2,1,0:T(8,128)(2,1)} %param.6, f32[512]{0:T(512)S(1)} %bitcast.223, bf16[8,1024,512]{2,1,0:T(8,128)(2,1)} %all-gather.9.cloned.1.call-done), kind=kOutput, calls=%fused_computation.40 | convolution fusion | flops 2152726528 | bytes 6293504 | tf_op jit(solution)/shard_map/dot_general | solution.py:71
  271.4 3.2 fusion.107
  274.6 2.5 copy.41
  277.2 5.9 %convolution_convert_fusion.7 = bf16[512,1024]{1,0:T(8,128)(2,1)} fusion(bf16[2,4,1024,1024]{3,2,1,0:T(8,128)(2,1)} %param.6, f32[512]{0:T(512)S(1)} %bitcast.224, bf16[8,1024,512]{2,1,0:T(8,128)(2,1)} %all-gather.9.cloned.1.call-done), kind=kOutput, calls=%fused_computation.42 | convolution fusion | flops 2152726528 | bytes 6293504 | tf_op jit(solution)/shard_map/dot_general | solution.py:71
  283.1 3.2 fusion.103
  286.3 2.5 copy.39
  288.8 5.9 %convolution_convert_fusion.6 = bf16[512,1024]{1,0:T(8,128)(2,1)} fusion(bf16[2,4,1024,1024]{3,2,1,0:T(8,128)(2,1)} %param.6, f32[512]{0:T(512)S(1)} %bitcast.225, bf16[8,1024,512]{2,1,0:T(8,128)(2,1)} %all-gather.9.cloned.1.call-done), kind=kOutput, calls=%fused_computation.41 | convolution fusion | flops 2152726528 | bytes 6293504 | tf_op jit(solution)/shard_map/dot_general | solution.py:71
  294.7 3.3 fusion.105
  298.0 2.5 copy.40
  300.6 3.7 %fusion.33 = f32[512,512]{1,0:T(8,128)S(1)} fusion(f32[512,512]{1,0:T(8,128)} %fusion.108, f32[512,512]{0,1:T(8,128)} %copy.46, f32[512,512]{1,0:T(8,128)} %fusion.106, f32[512,512]{0,1:T(8,128)} %copy.45, f32[512,512]{1,0:T(8,128)S(1)} %fusion.104, f32[512,512]{0,1:T(8,128)} %copy.44, f32[512,512]{1,0:T(8,128)S(1)} %fusion.102, f32[512,512]{0,1:T(8,128)S(1)} %copy.43, ...), kind=kLoop, calls=%fused_computation.57 | loop fusion | flops 2883584 | bytes 9437200 | tf_op jit(solution)/shard_map/add | solution.py:78
  304.4 0.2 copy-done.4
  304.6 0.3 copy-done.5
  304.9 0.3 copy-done.6
  305.2 0.3 copy-done.7
  305.5 1.0 fusion.40
  306.6 0.3 maximum_bitcast_fusion
  306.8 35.5 %all_to_all.5 = f32[32,2,16,512]{3,2,1,0:T(8,128)S(1)} all-to-all(f32[32,2,16,512]{3,2,1,0:T(8,128)S(1)} %maximum_bitcast_fusion), channel_id=1, replica_groups=mesh['tm'=4,'pair_0'=2,'pair_1'=4,'pair_2'=4] {'pair_0','pair_1','pair_2'}, dimensions={0} | all-to-all | bytes 4194304 | tf_op jit(solution)/shard_map/all_to_all | solution.py:39
  342.3 0.8 reduce_sum.9
  (26 shorter events, 0.1 us)
Async XLA Ops:
  6.5 43.8 %all-gather.5.cloned.1.call-start = ((), (), s32[]{:S(2)}) async-start(), calls=%async_computation.1 | async-start | bytes 2621440 | tf_op jit(solution)/shard_map/all_gather | solution.py:20
  17.5 117.6 %all-gather.7.cloned.1.call-start = ((), (), s32[]{:S(2)}) async-start(), calls=%async_computation.2 | async-start | bytes 10485760 | tf_op jit(solution)/shard_map/all_gather | solution.py:20
  50.4 163.0 %all-gather.9.cloned.1.call-start = ((), (), s32[]{:S(2)}) async-start(), calls=%async_computation.3 | async-start | bytes 10485760 | tf_op jit(solution)/shard_map/all_gather | solution.py:48
  147.0 1.7 copy-start.9
  147.0 1.7 copy-start.8
  300.5 3.8 %copy-start = (f32[512,512]{1,0:T(8,128)S(1)}, f32[512,512]{1,0:T(8,128)}, u32[]{:S(2)}) copy-start(f32[512,512]{1,0:T(8,128)} %fusion.109) | copy-start | bytes 3145732
  300.5 3.8 %copy-start.1 = (f32[512,512]{0,1:T(8,128)S(1)}, f32[512,512]{0,1:T(8,128)}, u32[]{:S(2)}) copy-start(f32[512,512]{0,1:T(8,128)} %copy.42) | copy-start | bytes 3145732
  300.5 3.8 %copy-start.2 = (f32[512,512]{1,0:T(8,128)S(1)}, f32[512,512]{1,0:T(8,128)}, u32[]{:S(2)}) copy-start(f32[512,512]{1,0:T(8,128)} %fusion.107) | copy-start | bytes 3145732
  300.5 3.8 %copy-start.3 = (f32[512,512]{0,1:T(8,128)S(1)}, f32[512,512]{0,1:T(8,128)}, u32[]{:S(2)}) copy-start(f32[512,512]{0,1:T(8,128)} %copy.41) | copy-start | bytes 3145732
  300.5 4.1 %copy-start.4 = (f32[512,512]{1,0:T(8,128)S(1)}, f32[512,512]{1,0:T(8,128)}, u32[]{:S(2)}) copy-start(f32[512,512]{1,0:T(8,128)} %fusion.103) | copy-start | bytes 3145732
  300.6 4.4 %copy-start.5 = (f32[512,512]{0,1:T(8,128)S(1)}, f32[512,512]{0,1:T(8,128)}, u32[]{:S(2)}) copy-start(f32[512,512]{0,1:T(8,128)} %copy.39) | copy-start | bytes 3145732
  300.6 4.7 %copy-start.6 = (f32[512,512]{1,0:T(8,128)S(1)}, f32[512,512]{1,0:T(8,128)}, u32[]{:S(2)}) copy-start(f32[512,512]{1,0:T(8,128)} %fusion.105) | copy-start | bytes 3145732
  300.6 4.9 %copy-start.7 = (f32[512,512]{0,1:T(8,128)S(1)}, f32[512,512]{0,1:T(8,128)}, u32[]{:S(2)}) copy-start(f32[512,512]{0,1:T(8,128)} %copy.40) | copy-start | bytes 3145732
Sparse Core Ops, SparseCore 0:
  17.6 32.7 all-gather.4
  52.0 83.0 all-gather.6
  148.8 64.5 all-gather.8
where the time goes:
time: 350 us
  waiting for transfers between devices  175 us (50%)
  matrix products  70 us (20%)
  blocking collectives  46.5 us (13%)
  local copies, waits for them, and re-layouts  31.8 us (9%)
  between operations  18.3 us (5%)
  other arithmetic  7.55 us (2%)
    all_gather x2, waiting for transfers between devices, stacked_from(): tiles = lax.all_gather(tiles, axes[k], axis=0, tiled=True)  117 us
    all_gather x1, waiting for transfers between devices, shards(): chosen = lax.all_gather(picked, 'tm', axis=2, tiled=True)  58.9 us
    dot_general x8, matrix products, shards(): lax.dot_general(left, product, (((0,), (0,)), ((), ())), preferred_elemen...  46.3 us
    all_to_all x1, blocking collectives, sum_at_owner(): tiles = lax.all_to_all(split_up(array, dim, count), axis, 0, 0, tiled=True)  35.5 us
    dot_general x8, matrix products, shards(): block = jnp.dot(half, right, preferred_element_type=jnp.float32)  23.6 us
    dot_general x8, local copies, waits for them, and re-layouts, shards(): block = jnp.dot(half, right, preferred_element_type=jnp.float32)  17.2 us
    all_gather x1, blocking collectives, stacked_from(): tiles = lax.all_gather(tiles, axes[k], axis=0, tiled=True)  10.9 us
    transpose x1, local copies, waits for them, and re-layouts, stacked_from(): tiles.transpose(*turned, *range(len(sequence), tiles.ndim))  7.53 us
  transfers between devices with their start and end apart: 3, of which 3 were waited for; matrix products, arithmetic and copies ran while one was open for 0% of the time, Pallas kernels for 0%

commit v1 on v0

--- a/solution.py
+++ b/solution.py
@@ -45,7 +45,9 @@
     wanted = pair_blocks.reshape(-1)
     narrow = whole_of(orbitals, PAIR, (0, 1, 2), 0)
     picked = jnp.take(narrow.reshape(-1, block_rows, narrow.shape[1]), wanted, axis=0)
-    chosen = lax.all_gather(picked, "tm", axis=2, tiled=True)
+    chosen = jnp.concatenate(
+        lax.all_to_all(jnp.stack([picked] * lax.axis_size("tm")), "tm", 0, 0), axis=2
+    )
     orbital_count = chosen.shape[2]
     time_local = screened.shape[0]
     pair_local = screened.shape[1]

time: 350 us -> 419 us (1.20)
  local copies, waits for them, and re-layouts: 31.8 us -> 64.2 us
  waiting for transfers between devices: 175 us -> 205 us
  starting transfers between devices: 0.08 us -> 6.05 us
    all_to_all x0 -> x1, waiting for transfers between devices: none -> 88.7 us  [shards(): lax.all_to_all(jnp.stack([picked] * lax.axis_size('tm')), 'tm', 0, 0)]
    all_gather x1 -> x0, waiting for transfers between devices: 58.9 us -> none  [shards(): chosen = lax.all_gather(picked, 'tm', axis=2, tiled=True)]
    slice x0 -> x9, local copies, waits for them, and re-layouts: none -> 20.1 us  [the longest x5 11 us: shards(): right = chosen[2 * pair_step + 1]]
    all_to_all x0 -> x1, local copies, waits for them, and re-layouts: none -> 7.53 us  [shards(): lax.all_to_all(jnp.stack([picked] * lax.axis_size('tm')), 'tm', 0, 0)]
    all_to_all x0 -> x1, starting transfers between devices: none -> 6 us  [shards(): lax.all_to_all(jnp.stack([picked] * lax.axis_size('tm')), 'tm', 0, 0)]
    another operation x0 -> x1, local copies, waits for them, and re-layouts: none -> 5.43 us  [shards(): jnp.stack([picked] * lax.axis_size('tm'))]
where the time goes in v1:
time: 419 us; the launch traced here: 418 us
  waiting for transfers between devices  205 us (49%)
  matrix products  71 us (17%)
  local copies, waits for them, and re-layouts  64.2 us (15%)
  blocking collectives  46.3 us (11%)
  between operations  18.6 us (4%)
  other arithmetic  6.78 us (2%)
  starting transfers between devices  6.05 us (1%)
    all_gather x2, waiting for transfers between devices, stacked_from(): tiles = lax.all_gather(tiles, axes[k], axis=0, tiled=True)  117 us
    all_to_all x1, waiting for transfers between devices, shards(): lax.all_to_all(jnp.stack([picked] * lax.axis_size('tm')), 'tm', 0, 0)  88.7 us
    dot_general x8, matrix products, shards(): lax.dot_general(left, product, (((0,), (0,)), ((), ())), preferred_elemen...  47.4 us
    all_to_all x1, blocking collectives, sum_at_owner(): tiles = lax.all_to_all(split_up(array, dim, count), axis, 0, 0, tiled=True)  35.4 us
    dot_general x8, matrix products, shards(): block = jnp.dot(half, right, preferred_element_type=jnp.float32)  23.6 us
    dot_general x8, local copies, waits for them, and re-layouts, shards(): block = jnp.dot(half, right, preferred_element_type=jnp.float32)  17.1 us
    slice x5, local copies, waits for them, and re-layouts, shards(): right = chosen[2 * pair_step + 1]  11 us
    all_gather x1, blocking collectives, stacked_from(): tiles = lax.all_gather(tiles, axes[k], axis=0, tiled=True)  10.9 us
  transfers between devices with their start and end apart: 3, of which 3 were waited for; matrix products, arithmetic and copies ran while one was open for 0% of the time, Pallas kernels for 0%

profile of v1, /device:TPU:0, one launch (start us, length us, event | category | flops | bytes accessed | tf_op | source)
XLA Modules:
  0.0 418.3 jit_solution(1424760639636686576)
XLA Ops:
  6.5 10.9 %all-gather = bf16[2048,128]{1,0:T(8,128)(2,1)} all-gather(bf16[1024,128]{1,0:T(8,128)(2,1)} %param.4), channel_id=2, replica_groups=mesh['tm'=4,'pair_0'=2,'pair_1'=4,'pair_2'=4] {'pair_0'}, dimensions={0}, use_global_device_ids=true | all-gather | bytes 786432 | tf_op jit(solution)/shard_map/all_gather | solution.py:20
  17.6 32.8 %all-gather.4.cloned.1.call-done = bf16[8,1024,128]{2,1,0:T(8,128)(2,1)} async-done(((bf16[2,1024,128]{2,1,0:T(8,128)(2,1)}), bf16[8,1024,128]{2,1,0:T(8,128)(2,1)}) %all-gather.4.cloned.1.call-update) | async-done | bytes 2097168 | tf_op jit(solution)/shard_map/all_gather | solution.py:20
  50.4 0.8 copy.45
  51.4 83.7 %all-gather.6.cloned.1.call-done = bf16[32,1024,128]{2,1,0:T(8,128)(2,1)} async-done(((bf16[8,1024,128]{2,1,0:T(8,128)(2,1)}), bf16[32,1024,128]{2,1,0:T(8,128)(2,1)}) %all-gather.6.cloned.1.call-update) | async-done | bytes 8388624 | tf_op jit(solution)/shard_map/all_gather | solution.py:20
  135.1 7.5 %copy.46 = bf16[2,4,4,1024,128]{4,3,2,1,0:T(8,128)(2,1)} copy(bf16[2,4,4,1024,128]{4,3,0,1,2:T(8,128)(2,1)} %bitcast.270) | data formatting | bytes 16777216 | tf_op jit(solution)/shard_map/transpose | solution.py:24
  142.6 4.3 %gather_fusion = bf16[8,1024,128]{2,1,0:T(8,128)(2,1)S(1)} fusion(bf16[32,1024,128]{2,1,0:T(8,128)(2,1)} %bitcast.269, s32[1024]{0:T(1024)S(1)} %pad_clamp_fusion), kind=kCustom, calls=%fused_computation | custom fusion | bytes 4194336 | tf_op jit(solution)/shard_map/jit(_take)/gather | solution.py:47
  147.2 5.4 %stack.16 = bf16[4,8,1024,128]{3,2,1,0:T(8,128)(2,1)} broadcast(bf16[8,1024,128]{2,1,0:T(8,128)(2,1)S(1)} %broadcast_select_fusion), dimensions={1,2,3} | broadcast | bytes 10485760 | tf_op jit(solution)/shard_map/stack | solution.py:49
  152.7 6.0 %all-to-all-start = ((bf16[4,8,1024,128]{3,2,1,0:T(8,128)(2,1)}), bf16[4,8,1024,128]{3,2,1,0:T(8,128)(2,1)}, u32[]{:S(2)}, u32[]{:S(2)}) async-start(bf16[4,8,1024,128]{3,2,1,0:T(8,128)(2,1)} %stack.16), calls=%async_computation | async-start | bytes 16777216 | tf_op jit(solution)/shard_map/all_to_all | solution.py:49
  158.7 0.7 fusion.138
  164.5 88.7 %all-to-all-done = bf16[4,8,1024,128]{3,2,1,0:T(8,128)(2,1)} async-done(((bf16[4,8,1024,128]{3,2,1,0:T(8,128)(2,1)}), bf16[4,8,1024,128]{3,2,1,0:T(8,128)(2,1)}, u32[]{:S(2)}, u32[]{:S(2)}) %all-to-all-start) | async-done | bytes 8388640 | tf_op jit(solution)/shard_map/all_to_all | solution.py:49
  253.1 7.5 %copy.68 = bf16[4,8,1024,128]{3,2,0,1:T(8,128)(2,1)} copy(bf16[4,8,1024,128]{3,2,1,0:T(8,128)(2,1)} %all-to-all-done) | data formatting | bytes 16777216 | tf_op jit(solution)/shard_map/all_to_all | solution.py:49
  260.7 5.6 %fusion.136 = (bf16[1,1024,4,128]{3,1,2,0:T(8,128)(2,1)S(1)}, bf16[1,1024,4,128]{3,1,2,0:T(8,128)(2,1)S(1)}, bf16[1,1024,4,128]{3,1,2,0:T(8,128)(2,1)}, bf16[1,1...) fusion(bf16[8,1024,4,128]{3,1,2,0:T(8,128)(2,1)} %bitcast.260), kind=kLoop, calls=%fused_computation.115 | loop fusion | bytes 16777216 | tf_op jit(solution)/shard_map/slice | solution.py:65
  266.3 2.3 copy.58
  268.6 5.9 %convolution_convert_fusion = bf16[512,1024]{1,0:T(8,128)(2,1)} fusion(bf16[1024,512]{0,1:T(8,128)(2,1)} %bitcast.284, bf16[2,4,1024,1024]{3,2,1,0:T(8,128)(2,1)} %param.6, f32[4,128]{1,0:T(4,128)S(1)} %bitcast.294, bf16[8,1024,4,128]{3,1,2,0:T(8,128)(2,1)} %bitcast.261), kind=kOutput, calls=%fused_computation.36 | convolution fusion | flops 2152726528 | bytes 6293504 | tf_op jit(solution)/shard_map/dot_general | solution.py:73
  274.5 5.9 %convolution_convert_fusion.4 = bf16[512,1024]{1,0:T(8,128)(2,1)} fusion(bf16[1024,512]{0,1:T(8,128)(2,1)} %bitcast.285, bf16[2,4,1024,1024]{3,2,1,0:T(8,128)(2,1)} %param.6, f32[4,128]{1,0:T(4,128)S(1)} %bitcast.290, bf16[8,1024,4,128]{3,1,2,0:T(8,128)(2,1)} %bitcast.262), kind=kOutput, calls=%fused_computation.40 | convolution fusion | flops 2152726528 | bytes 6293504 | tf_op jit(solution)/shard_map/dot_general | solution.py:73
  280.4 2.3 copy.55
  282.7 5.9 %convolution_convert_fusion.1 = bf16[512,1024]{1,0:T(8,128)(2,1)} fusion(bf16[1024,512]{0,1:T(8,128)(2,1)} %bitcast.286, bf16[2,4,1024,1024]{3,2,1,0:T(8,128)(2,1)} %param.6, f32[4,128]{1,0:T(4,128)S(1)} %bitcast.295, bf16[8,1024,4,128]{3,1,2,0:T(8,128)(2,1)} %bitcast.263), kind=kOutput, calls=%fused_computation.37 | convolution fusion | flops 2152726528 | bytes 6293504 | tf_op jit(solution)/shard_map/dot_general | solution.py:73
  288.6 5.9 %convolution_convert_fusion.5 = bf16[512,1024]{1,0:T(8,128)(2,1)} fusion(bf16[1024,512]{0,1:T(8,128)(2,1)} %bitcast.287, bf16[2,4,1024,1024]{3,2,1,0:T(8,128)(2,1)} %param.6, f32[4,128]{1,0:T(4,128)S(1)} %bitcast.291, bf16[8,1024,4,128]{3,1,2,0:T(8,128)(2,1)} %bitcast.264), kind=kOutput, calls=%fused_computation.41 | convolution fusion | flops 2152726528 | bytes 6293504 | tf_op jit(solution)/shard_map/dot_general | solution.py:73
  294.5 2.3 copy.52
  296.8 5.9 %convolution_convert_fusion.2 = bf16[512,1024]{1,0:T(8,128)(2,1)} fusion(bf16[1024,512]{0,1:T(8,128)(2,1)} %bitcast.288, bf16[2,4,1024,1024]{3,2,1,0:T(8,128)(2,1)} %param.6, f32[4,128]{1,0:T(4,128)S(1)} %bitcast.296, bf16[8,1024,4,128]{3,1,2,0:T(8,128)(2,1)} %bitcast.265), kind=kOutput, calls=%fused_computation.38 | convolution fusion | flops 2152726528 | bytes 6293504 | tf_op jit(solution)/shard_map/dot_general | solution.py:73
  302.7 6.0 %convolution_convert_fusion.6 = bf16[512,1024]{1,0:T(8,128)(2,1)} fusion(bf16[1024,512]{0,1:T(8,128)(2,1)} %bitcast.289, bf16[2,4,1024,1024]{3,2,1,0:T(8,128)(2,1)} %param.6, f32[4,128]{1,0:T(4,128)S(1)} %bitcast.292, bf16[8,1024,4,128]{3,1,2,0:T(8,128)(2,1)} %bitcast.266), kind=kOutput, calls=%fused_computation.42 | convolution fusion | flops 2152726528 | bytes 6293504 | tf_op jit(solution)/shard_map/dot_general | solution.py:73
  308.7 2.3 copy.49
  310.9 6.0 %convolution_convert_fusion.3 = bf16[512,1024]{1,0:T(8,128)(2,1)} fusion(bf16[1024,512]{0,1:T(8,128)(2,1)} %bitcast.276, bf16[2,4,1024,1024]{3,2,1,0:T(8,128)(2,1)} %param.6, f32[4,128]{1,0:T(4,128)S(1)} %bitcast.297, bf16[8,1024,4,128]{3,1,2,0:T(8,128)(2,1)} %bitcast.267), kind=kOutput, calls=%fused_computation.39 | convolution fusion | flops 2152726528 | bytes 6293504 | tf_op jit(solution)/shard_map/dot_general | solution.py:73
  316.9 5.9 %convolution_convert_fusion.7 = bf16[512,1024]{1,0:T(8,128)(2,1)} fusion(bf16[1024,512]{0,1:T(8,128)(2,1)} %bitcast.277, bf16[2,4,1024,1024]{3,2,1,0:T(8,128)(2,1)} %param.6, f32[4,128]{1,0:T(4,128)S(1)} %bitcast.293, bf16[8,1024,4,128]{3,1,2,0:T(8,128)(2,1)} %bitcast.268), kind=kOutput, calls=%fused_computation.43 | convolution fusion | flops 2152726528 | bytes 6293504 | tf_op jit(solution)/shard_map/dot_general | solution.py:73
  322.8 1.3 copy.50
  324.1 0.5 copy.59
  324.7 2.9 fusion.146
  327.6 2.0 fusion.142
  329.6 0.3 copy.60
  329.9 2.5 copy.64
  332.4 2.3 copy.56
  334.7 3.3 fusion.145
  338.0 3.3 fusion.141
  341.3 2.5 copy.57
  343.8 2.6 copy.63
  346.4 1.3 copy.53
  347.7 3.3 fusion.144
  351.0 2.3 fusion.140
  353.3 1.3 copy.54
  354.6 2.6 copy.62
  357.2 3.3 fusion.139
  360.5 3.3 fusion.143
  363.8 2.6 copy.61
  366.4 2.6 copy.51
  369.0 4.3 %fusion.33 = f32[512,512]{1,0:T(8,128)S(1)} fusion(f32[512,512]{1,0:T(8,128)S(1)} %copy-done.2, f32[512,512]{0,1:T(8,128)} %copy.64, f32[512,512]{1,0:T(8,128)} %fusion.145, f32[512,512]{0,1:T(8,128)} %copy.63, f32[512,512]{1,0:T(8,128)} %fusion.144, f32[512,512]{0,1:T(8,128)} %copy.62, f32[512,512]{1,0:T(8,128)} %fusion.143, f32[512,512]{0,1:T(8,128)} %copy.61, ...), kind=kLoop, calls=%fused_computation.54 | loop fusion | flops 2883584 | bytes 9437200 | tf_op jit(solution)/shard_map/add | solution.py:80
  374.0 1.0 fusion.40
  375.3 35.4 %all_to_all.10 = f32[32,2,16,512]{3,2,1,0:T(8,128)S(1)} all-to-all(f32[32,2,16,512]{3,2,1,0:T(8,128)S(1)} %maximum_bitcast_fusion), channel_id=1, replica_groups=mesh['tm'=4,'pair_0'=2,'pair_1'=4,'pair_2'=4] {'pair_0','pair_1','pair_2'}, dimensions={0} | all-to-all | bytes 4194304 | tf_op jit(solution)/shard_map/all_to_all | solution.py:39
  410.7 0.8 reduce_sum.9
  (36 shorter events, 1.5 us)
Async XLA Ops:
  6.5 43.8 %all-gather.4.cloned.1.call-start = ((), (), s32[]{:S(2)}) async-start(), calls=%async_computation.2 | async-start | bytes 2621440 | tf_op jit(solution)/shard_map/all_gather | solution.py:20
  17.5 117.6 %all-gather.6.cloned.1.call-start = ((), (), s32[]{:S(2)}) async-start(), calls=%async_computation.3 | async-start | bytes 10485760 | tf_op jit(solution)/shard_map/all_gather | solution.py:20
  152.7 6.0 %copy-start.9 = (f32[512]{0:T(512)S(1)}, f32[512]{0:T(512)}, u32[]{:S(2)}) copy-start(f32[512]{0:T(512)} %param.5) | copy-start | bytes 6148
  152.7 6.0 %copy-start.8 = (s32[4,2]{0,1:T(2,128)S(1)}, s32[4,2]{0,1:T(2,128)}, u32[]{:S(2)}) copy-start(s32[4,2]{0,1:T(2,128)} %param.7) | copy-start | bytes 100
  152.7 100.5 %all-to-all-start = ((bf16[4,8,1024,128]{3,2,1,0:T(8,128)(2,1)}), bf16[4,8,1024,128]{3,2,1,0:T(8,128)(2,1)}, u32[]{:S(2)}, u32[]{:S(2)}) async-start(bf16[4,8,1024,128]{3,2,1,0:T(8,128)(2,1)} %stack.16), calls=%async_computation | async-start | bytes 16777216 | tf_op jit(solution)/shard_map/all_to_all | solution.py:49
  353.3 3.9 copy-start.3
  360.5 8.5 %copy-start.2 = (f32[512,512]{1,0:T(8,128)S(1)}, f32[512,512]{1,0:T(8,128)}, u32[]{:S(2)}) copy-start(f32[512,512]{1,0:T(8,128)} %fusion.146) | copy-start | bytes 3145732
  369.0 4.4 %copy-start = (f32[512,512]{1,0:T(8,128)S(1)}, f32[512,512]{1,0:T(8,128)}, u32[]{:S(2)}) copy-start(f32[512,512]{1,0:T(8,128)} %fusion.141) | copy-start | bytes 3145732
  369.0 4.4 %copy-start.1 = (f32[512,512]{0,1:T(8,128)S(1)}, f32[512,512]{0,1:T(8,128)}, u32[]{:S(2)}) copy-start(f32[512,512]{0,1:T(8,128)} %copy.57) | copy-start | bytes 3145732
  369.0 4.4 %copy-start.4 = (f32[512,512]{1,0:T(8,128)S(1)}, f32[512,512]{1,0:T(8,128)}, u32[]{:S(2)}) copy-start(f32[512,512]{1,0:T(8,128)} %copy-done.3) | copy-start | bytes 3145732
  369.0 4.4 %copy-start.5 = (f32[512,512]{0,1:T(8,128)S(1)}, f32[512,512]{0,1:T(8,128)}, u32[]{:S(2)}) copy-start(f32[512,512]{0,1:T(8,128)} %copy.54) | copy-start | bytes 3145732
  369.0 4.6 %copy-start.6 = (f32[512,512]{1,0:T(8,128)S(1)}, f32[512,512]{1,0:T(8,128)}, u32[]{:S(2)}) copy-start(f32[512,512]{1,0:T(8,128)} %fusion.139) | copy-start | bytes 3145732
  369.0 4.9 %copy-start.7 = (f32[512,512]{0,1:T(8,128)S(1)}, f32[512,512]{0,1:T(8,128)}, u32[]{:S(2)}) copy-start(f32[512,512]{0,1:T(8,128)} %copy.51) | copy-start | bytes 3145732
Sparse Core Ops, SparseCore 0:
  17.6 32.7 all-gather.3
  52.0 83.0 all-gather.5
